TPU v7x, 32 devices: a whole 2x2x4 slice. The times are simulated.
32 devices in a mesh: parts: 2 (over y), blk: 4 (over z), grp: 4 (over x, core).
Axes of the slice: x: 2, y: 2, z: 4, core: 2. Of those that a mesh axis runs over, the one named last changes fastest.
Arguments:
- factors: float32 [64, 4096], P(None, ('parts', 'blk', 'grp')), parts along dimension 1, may hold values from -1 to 1
- tangent: float32 [64, 4096], P(None, ('parts', 'blk', 'grp')), parts along dimension 1, may hold values from -15 to 15
- counts: int32 [4096, 2048], P(('parts', 'blk', 'grp')), parts along dimension 0, may hold values from 0 to 4, as said below
Outputs:
- hess_vec: float32 [64, 4096], P(None, ('parts', 'blk', 'grp')), parts along dimension 1
- residual: float32 [64, 4096], P(None, ('parts', 'blk', 'grp')), parts along dimension 1
- inner: float32 [4], P('parts'), parts along dimension 0
There are 2 independent parts, one for each index of `parts`. A program takes and returns all parts, laid end to end along the dimension named above; each array names one. Nothing has to cross between parts.
Inputs may be any that keep to these rules, and one draw needn't show every extreme that they name: counts is symmetric.
All inputs are finite; a program needn't handle non-finite values.
Results may differ from a plain program's by a relative error of at most 0.0003.
Values sent between devices are 32-bit elements; how exact they have to be, the bound alone decides.
A program may use at most 128 MiB of HBM per device.

v0:
```python
import jax
import jax.numpy as jnp
from jax import lax
from jax.sharding import PartitionSpec as P


def local(factors, tangent, counts):
    rows = counts.shape[0]
    nodes = counts.shape[1]
    scale = 1.0 / jnp.sqrt(jnp.float32(nodes))
    highest = lax.Precision.HIGHEST
    contract = (((0,), (0,)), ((), ()))
    right = (((1,), (1,)), ((), ()))
    row_start = (lax.axis_index("blk") * lax.axis_size("grp") + lax.axis_index("grp")) * rows
    row_ids = row_start + jnp.arange(rows, dtype=jnp.int32)[:, None]
    group_u, group_v = (
        lax.all_gather(factors, "grp", axis=1, tiled=True),
        lax.all_gather(tangent, "grp", axis=1, tiled=True),
    )
    piece_u = lax.all_gather(group_u, "blk", axis=1, tiled=True)
    piece_v = lax.all_gather(group_v, "blk", axis=1, tiled=True)
    width = piece_u.shape[1]
    eta = lax.dot_general(factors, piece_u, contract, precision=highest)
    deta = lax.dot_general(factors, piece_v, contract, precision=highest) + lax.dot_general(
        tangent, piece_u, contract, precision=highest
    )
    col_ids = jnp.arange(width, dtype=jnp.int32)[None, :]
    keep = row_ids != col_ids
    rate = jnp.where(keep, jnp.exp(eta), jnp.float32(0.0))
    weight = rate * deta
    tile_counts = counts.astype(jnp.float32)
    slack = jnp.where(keep, tile_counts - rate, jnp.float32(0.0))
    hess_acc = lax.dot_general(piece_u, weight, right, precision=highest)
    resid_acc = lax.dot_general(piece_u, slack - weight, right, precision=highest)
    hess_acc, resid_acc = (hess_acc, resid_acc)
    hess_vec = hess_acc * scale
    residual = resid_acc * scale
    sum_sq, sum_curv = lax.psum(
        (jnp.sum(residual * residual), jnp.sum(tangent * hess_vec)), ("blk", "grp")
    )
    inner = jnp.stack([sum_sq, sum_curv])
    return (hess_vec, residual, inner)


def solution(mesh):
    return jax.shard_map(
        local,
        mesh=mesh,
        in_specs=(
            P(None, ("parts", "blk", "grp")),
            P(None, ("parts", "blk", "grp")),
            P(("parts", "blk", "grp"), None),
        ),
        out_specs=(P(None, ("parts", "blk", "grp")), P(None, ("parts", "blk", "grp")), P("parts")),
        check_vma=False,
    )
```

profile of v0, /device:TPU:0, one launch (start us, length us, event | category | flops | bytes accessed | tf_op | source)
XLA Modules:
  0.0 85.9 jit_solution(17943244656120877728)
XLA Ops:
  0.6 0.0 copy-start.1
  0.7 6.7 %all_gather.12 = f32[64,512]{1,0:T(8,128)S(1)} all-gather(f32[64,128]{1,0:T(8,128)} %param.3), channel_id=1, replica_groups=mesh['parts'=2,'blk'=4,'grp'=4] {'grp'}, dimensions={1}, use_global_device_ids=true | all-gather | bytes 163840 | tf_op jit(solution)/shard_map/all_gather | solution.py:17
  7.4 0.0 copy-done.1
  7.4 5.6 %all_gather.14 = f32[64,512]{1,0:T(8,128)S(1)} all-gather(f32[64,128]{1,0:T(8,128)S(1)} %copy-done.1), channel_id=1, replica_groups=mesh['parts'=2,'blk'=4,'grp'=4] {'grp'}, dimensions={1}, use_global_device_ids=true | all-gather | bytes 163840 | tf_op jit(solution)/shard_map/all_gather | solution.py:18
  12.9 16.6 %all_gather.13 = f32[64,2048]{1,0:T(8,128)S(1)} all-gather(f32[64,512]{1,0:T(8,128)S(1)} %all_gather.12), channel_id=1, replica_groups=mesh['parts'=2,'blk'=4,'grp'=4] {'blk'}, dimensions={1}, use_global_device_ids=true | all-gather | bytes 655360 | tf_op jit(solution)/shard_map/all_gather | solution.py:20
  29.5 0.0 copy-start.2
  29.5 16.0 %all_gather.15 = f32[64,2048]{1,0:T(8,128)S(1)} all-gather(f32[64,512]{1,0:T(8,128)S(1)} %all_gather.14), channel_id=1, replica_groups=mesh['parts'=2,'blk'=4,'grp'=4] {'blk'}, dimensions={1}, use_global_device_ids=true | all-gather | bytes 655360 | tf_op jit(solution)/shard_map/all_gather | solution.py:21
  45.5 0.0 copy-done.2
  45.5 1.0 %fusion.11 = f32[128,2048]{1,0:T(8,128)S(1)} fusion(f32[64,128]{1,0:T(8,128)S(1)} %copy-done.2, f32[64,2048]{1,0:T(8,128)S(1)} %all_gather.15), kind=kOutput, calls=%fused_computation.20 | convolution fusion | flops 201326592 | bytes 1605632 | tf_op jit(solution)/shard_map/dot_general | solution.py:24
  46.6 1.1 %fusion.1 = f32[128,2048]{1,0:T(8,128)S(1)} fusion(f32[64,128]{1,0:T(8,128)S(1)} %copy-done.2, f32[64,2048]{1,0:T(8,128)S(1)} %all_gather.13, s32[128]{0:T(128)S(1)} %iota_add_fusion), kind=kOutput, calls=%fused_computation.3 | convolution fusion | flops 201850880 | bytes 1606144 | tf_op jit(solution)/shard_map/dot_general | solution.py:23
  47.7 0.0 copy-start
  47.7 1.1 %fusion = f32[128,2048]{1,0:T(8,128)S(1)} fusion(f32[128,2048]{1,0:T(8,128)S(1)} %fusion.1, f32[128,2048]{1,0:T(8,128)S(1)} %fusion.11, f32[64,128]{1,0:T(8,128)S(1)} %copy-done.1, f32[64,2048]{1,0:T(8,128)S(1)} %all_gather.13), kind=kOutput, calls=%fused_computation.1 | convolution fusion | flops 201850880 | bytes 3702784 | tf_op jit(solution)/shard_map/dot_general | solution.py:24
  48.8 0.2 copy-done
  48.9 2.7 %multiply_reduce_fusion.1 = (f32[]{:T(128)}, f32[64,128]{1,0:T(8,128)}) fusion(f32[64,2048]{1,0:T(8,128)S(1)} %all_gather.13, f32[128,2048]{1,0:T(8,128)S(1)} %fusion, f32[128,2048]{1,0:T(8,128)S(1)} %fusion.1, s32[128,2048]{1,0:T(8,128)S(1)} %copy-done, s32[128]{0:T(128)S(1)} %iota_add_fusion), kind=kOutput, calls=%fused_computation.16 | convolution fusion | flops 202661888 | bytes 3703300 | tf_op jit(solution)/shard_map/dot_general | solution.py:34
  51.6 2.4 %multiply_reduce_fusion = (f32[]{:T(128)}, f32[64,128]{1,0:T(8,128)}) fusion(f32[64,128]{1,0:T(8,128)S(1)} %copy-done.1, f32[128,2048]{1,0:T(8,128)S(1)} %fusion, f32[64,2048]{1,0:T(8,128)S(1)} %all_gather.13), kind=kOutput, calls=%fused_computation.15 | convolution fusion | flops 201351168 | bytes 1638404 | tf_op jit(solution)/shard_map/dot_general | solution.py:33
  54.0 30.1 %all-reduce = (f32[1]{0:T(128)}, f32[1]{0:T(128)}) all-reduce(f32[1]{0:T(128)} %bitcast.3, f32[1]{0:T(128)} %bitcast.2), channel_id=1, replica_groups=mesh['parts'=2,'blk'=4,'grp'=4] {'blk','grp'}, use_global_device_ids=true, to_apply=%region_3.4 | all-reduce | flops 2 | bytes 16 | tf_op jit(solution)/shard_map/psum | solution.py:38
  84.2 1.8 %pad_maximum_fusion = f32[2]{0:T(128)} fusion(f32[1]{0:T(128)} %get-tuple-element.3, f32[1]{0:T(128)} %get-tuple-element.4), kind=kLoop, calls=%fused_computation.17 | loop fusion | flops 2 | bytes 16 | tf_op jit(solution)/shard_map/stack | solution.py:41
  (1 shorter events, 0.0 us)
Async XLA Ops:
  0.6 6.7 %copy-start.1 = (f32[64,128]{1,0:T(8,128)S(1)}, f32[64,128]{1,0:T(8,128)}, u32[]{:S(2)}) copy-start(f32[64,128]{1,0:T(8,128)} %param.4) | copy-start | bytes 98308
  29.5 16.0 %copy-start.2 = (f32[64,128]{1,0:T(8,128)S(1)}, f32[64,128]{1,0:T(8,128)}, u32[]{:S(2)}) copy-start(f32[64,128]{1,0:T(8,128)} %param.3) | copy-start | bytes 98308
  47.7 1.2 %copy-start = (s32[128,2048]{1,0:T(8,128)S(1)}, s32[128,2048]{1,0:T(8,128)}, u32[]{:S(2)}) copy-start(s32[128,2048]{1,0:T(8,128)} %param.5) | copy-start | bytes 3145732
where the time goes:
time: 86.3 us; the launch traced here: 85.9 us
  blocking collectives  75 us (87%)
  matrix products  8.3 us (10%)
  other arithmetic  1.78 us (2%)
    psum x1, blocking collectives, local(): lax.psum((jnp.sum(residual * residual), jnp.sum(tangent * hess_vec)), ('b...  30.1 us
    all_gather x1, blocking collectives, local(): piece_u = lax.all_gather(group_u, 'blk', axis=1, tiled=True)  16.6 us
    all_gather x1, blocking collectives, local(): piece_v = lax.all_gather(group_v, 'blk', axis=1, tiled=True)  16 us
    all_gather x1, blocking collectives, local(): lax.all_gather(factors, 'grp', axis=1, tiled=True)  6.69 us
    all_gather x1, blocking collectives, local(): lax.all_gather(tangent, 'grp', axis=1, tiled=True)  5.58 us
    dot_general x1, matrix products, local(): lax.dot_general(piece_u, slack - weight, right, precision=highest)  2.69 us
    dot_general x1, matrix products, local(): hess_acc = lax.dot_general(piece_u, weight, right, precision=highest)  2.41 us
    another operation x1, other arithmetic, local(): inner = jnp.stack([sum_sq, sum_curv])  1.78 us

commit v1 on v0

--- a/solution.py
+++ b/solution.py
@@ -2,6 +2,27 @@
 import jax.numpy as jnp
 from jax import lax
 from jax.sharding import PartitionSpec as P
+
+
+def gather_around(value, axis, dim):
+    devices, place, span = (lax.axis_size(axis), lax.axis_index(axis), value.shape[dim])
+    right = [(i, (i + 1) % devices) for i in range(devices)]
+    left = [(i, (i - 1) % devices) for i in range(devices)]
+    out = jnp.zeros((*value.shape[:dim], devices * span, *value.shape[dim + 1 :]), value.dtype)
+    out = lax.dynamic_update_slice_in_dim(out, value, place * span, axis=dim)
+    from_left = from_right = value
+    half = devices // 2
+    for turn in range(1, half + 1):
+        from_left = lax.ppermute(from_left, axis, right)
+        out = lax.dynamic_update_slice_in_dim(
+            out, from_left, (place - turn) % devices * span, axis=dim
+        )
+        if turn < devices - half:
+            from_right = lax.ppermute(from_right, axis, left)
+            out = lax.dynamic_update_slice_in_dim(
+                out, from_right, (place + turn) % devices * span, axis=dim
+            )
+    return out
 
 
 def local(factors, tangent, counts):
@@ -14,7 +35,7 @@
     row_start = (lax.axis_index("blk") * lax.axis_size("grp") + lax.axis_index("grp")) * rows
     row_ids = row_start + jnp.arange(rows, dtype=jnp.int32)[:, None]
     group_u, group_v = (
-        lax.all_gather(factors, "grp", axis=1, tiled=True),
+        gather_around(factors, "grp", 1),
         lax.all_gather(tangent, "grp", axis=1, tiled=True),
     )
     piece_u = lax.all_gather(group_u, "blk", axis=1, tiled=True)

time: 86.3 us -> 87.3 us (1.012)
  blocking collectives: 75 us -> 68.6 us
  waiting for transfers between devices: 0 us -> 3.29 us
  starting transfers between devices: 0 us -> 2.55 us
  matrix products: 8.3 us -> 9.54 us
    all_gather x1 -> x0, blocking collectives: 6.69 us -> none  [local(): lax.all_gather(factors, 'grp', axis=1, tiled=True)]
    ppermute x0 -> x3, waiting for transfers between devices: none -> 3.29 us  [the longest x2 3.28 us: gather_around(): from_left = lax.ppermute(from_left, axis, right)]
    ppermute x0 -> x3, starting transfers between devices: none -> 2.55 us  [the longest x1 1.99 us: gather_around(): from_right = lax.ppermute(from_right, axis, left)]
    all_gather x1, blocking collectives: 16.6 us -> 15.6 us  [local(): piece_u = lax.all_gather(group_u, 'blk', axis=1, tiled=True)]
  transfers between devices with their start and end apart: 0 -> 3, of which waited for: 0 -> 1; matrix products, arithmetic and copies ran while one was open for 0% -> 3% of each run, Pallas kernels for 0% -> 0%
where the time goes in v1:
time: 87.3 us; the launch traced here: 87 us
  blocking collectives  68.6 us (79%)
  matrix products  9.54 us (11%)
  waiting for transfers between devices  3.29 us (4%)
  starting transfers between devices  2.55 us (3%)
  other arithmetic  1.85 us (2%)
    psum x1, blocking collectives, local(): lax.psum((jnp.sum(residual * residual), jnp.sum(tangent * hess_vec)), ('b...  30.2 us
    all_gather x1, blocking collectives, local(): piece_v = lax.all_gather(group_v, 'blk', axis=1, tiled=True)  16.9 us
    all_gather x1, blocking collectives, local(): piece_u = lax.all_gather(group_u, 'blk', axis=1, tiled=True)  15.6 us
    all_gather x1, blocking collectives, local(): lax.all_gather(tangent, 'grp', axis=1, tiled=True)  5.98 us
    ppermute x2, waiting for transfers between devices, gather_around(): from_left = lax.ppermute(from_left, axis, right)  3.28 us
    dot_general x1, matrix products, local(): lax.dot_general(piece_u, slack - weight, right, precision=highest)  2.15 us
    ppermute x1, starting transfers between devices, gather_around(): from_right = lax.ppermute(from_right, axis, left)  1.99 us
    dot_general x1, matrix products, local(): hess_acc = lax.dot_general(piece_u, weight, right, precision=highest)  1.95 us
  transfers between devices with their start and end apart: 3, of which 1 were waited for; matrix products, arithmetic and copies ran while one was open for 3% of the time, Pallas kernels for 0%

profile of v1, /device:TPU:0, one launch (start us, length us, event | category | flops | bytes accessed | tf_op | source)
XLA Modules:
  0.0 87.0 jit_solution(16059933205235583533)
XLA Ops:
  0.6 0.5 collective-permute-start
  1.1 2.0 %collective-permute-start.1 = (f32[64,128]{1,0:T(8,128)}, f32[64,128]{1,0:T(8,128)S(1)}, u32[]{:S(2)}, u32[]{:S(2)}) collective-permute-start(f32[64,128]{1,0:T(8,128)} %param.3), channel_id=1, source_target_pairs={{0,3},{1,0},{2,1},{3,2},{4,7},{5,4},{6,5},{7,6},{8,11},{9,8},{10,9... | collective-permute-start | bytes 98312 | tf_op jit(solution)/shard_map/ppermute | solution.py:21
  3.1 6.0 %all_gather.10 = f32[64,512]{1,0:T(8,128)S(1)} all-gather(f32[64,128]{1,0:T(8,128)} %param.4), channel_id=1, replica_groups=mesh['parts'=2,'blk'=4,'grp'=4] {'grp'}, dimensions={1}, use_global_device_ids=true | all-gather | bytes 163840 | tf_op jit(solution)/shard_map/all_gather | solution.py:39
  9.1 0.0 copy-start.2
  9.1 16.9 %all_gather.11 = f32[64,2048]{1,0:T(8,128)S(1)} all-gather(f32[64,512]{1,0:T(8,128)S(1)} %all_gather.10), channel_id=1, replica_groups=mesh['parts'=2,'blk'=4,'grp'=4] {'blk'}, dimensions={1}, use_global_device_ids=true | all-gather | bytes 655360 | tf_op jit(solution)/shard_map/all_gather | solution.py:42
  26.0 0.0 copy-done.2
  26.0 0.0 copy-start
  26.0 1.8 %fusion.11 = f32[128,2048]{0,1:T(8,128)S(1)} fusion(f32[64,128]{1,0:T(8,128)S(1)} %copy-done.2, f32[64,2048]{1,0:T(8,128)S(1)} %all_gather.11), kind=kOutput, calls=%fused_computation.24 | convolution fusion | flops 201326592 | bytes 1605632 | tf_op jit(solution)/shard_map/dot_general | solution.py:45
  27.9 0.0 copy-done
  27.9 0.3 copy.7
  28.3 0.0 collective-permute-done
  28.3 0.1 collective-permute-start.2
  28.4 0.0 collective-permute-done.1
  28.4 3.3 %collective-permute-done.2 = f32[64,128]{1,0:T(8,128)S(1)} collective-permute-done((f32[64,128]{1,0:T(8,128)S(1)}, f32[64,128]{1,0:T(8,128)S(1)}, u32[]{:S(2)}, u32[]{:S(2)}) %collective-permute-start.2) | collective-permute-done | bytes 32800 | tf_op jit(solution)/shard_map/ppermute | solution.py:16
  31.7 15.6 %all_gather.9 = f32[64,2048]{1,0:T(8,128)S(1)} all-gather(f32[64,512]{1,0:T(8,128)S(1)} %constant_dynamic-update-slice_fusion), channel_id=1, replica_groups=mesh['parts'=2,'blk'=4,'grp'=4] {'blk'}, dimensions={1}, use_global_device_ids=true | all-gather | bytes 655360 | tf_op jit(solution)/shard_map/all_gather | solution.py:41
  47.3 0.0 copy-start.1
  47.3 1.8 %fusion.3 = f32[128,2048]{0,1:T(8,128)S(1)} fusion(f32[64,2048]{1,0:T(8,128)S(1)} %all_gather.9, f32[64,128]{1,0:T(8,128)S(1)} %copy-done.2, s32[128]{0:T(128)S(1)} %iota_add_fusion), kind=kOutput, calls=%fused_computation.5 | convolution fusion | flops 201850880 | bytes 1606144 | tf_op jit(solution)/shard_map/dot_general | solution.py:44
  49.1 0.0 copy-done.1
  49.1 1.8 %fusion.1 = f32[128,2048]{0,1:T(8,128)S(1)} fusion(f32[128,2048]{0,1:T(8,128)S(1)} %fusion.3, f32[128,2048]{0,1:T(8,128)S(1)} %fusion.11, f32[64,2048]{1,0:T(8,128)S(1)} %all_gather.9, f32[64,128]{1,0:T(8,128)S(1)} %copy-done.1), kind=kOutput, calls=%fused_computation.2 | convolution fusion | flops 201850880 | bytes 3702784 | tf_op jit(solution)/shard_map/dot_general | solution.py:45
  50.9 2.0 %multiply_reduce_fusion = (f32[]{:T(128)}, f32[64,128]{1,0:T(8,128)}) fusion(f32[64,128]{1,0:T(8,128)S(1)} %copy-done.1, f32[64,2048]{1,0:T(8,128)S(1)} %all_gather.9, f32[128,2048]{0,1:T(8,128)S(1)} %fusion.1), kind=kOutput, calls=%fused_computation.15 | convolution fusion | flops 201351168 | bytes 1638404 | tf_op jit(solution)/shard_map/dot_general | solution.py:54
  52.9 2.2 %multiply_reduce_fusion.1 = (f32[]{:T(128)}, f32[64,128]{1,0:T(8,128)}) fusion(f32[64,2048]{1,0:T(8,128)S(1)} %all_gather.9, f32[128,2048]{0,1:T(8,128)S(1)} %fusion.1, f32[128,2048]{0,1:T(8,128)S(1)} %fusion.3, s32[128,2048]{0,1:T(8,128)S(1)} %copy.7, s32[128]{0:T(128)S(1)} %iota_add_fusion), kind=kOutput, calls=%fused_computation.16 | convolution fusion | flops 202661888 | bytes 3703300 | tf_op jit(solution)/shard_map/dot_general | solution.py:55
  55.0 30.2 %all-reduce = (f32[1]{0:T(128)}, f32[1]{0:T(128)}) all-reduce(f32[1]{0:T(128)} %bitcast.3, f32[1]{0:T(128)} %bitcast.2), channel_id=1, replica_groups=mesh['parts'=2,'blk'=4,'grp'=4] {'blk','grp'}, use_global_device_ids=true, to_apply=%region_3.4 | all-reduce | flops 2 | bytes 16 | tf_op jit(solution)/shard_map/psum | solution.py:59
  85.2 1.8 %pad_maximum_fusion = f32[2]{0:T(128)} fusion(f32[1]{0:T(128)} %get-tuple-element.3, f32[1]{0:T(128)} %get-tuple-element.4), kind=kLoop, calls=%fused_computation.21 | loop fusion | flops 2 | bytes 16 | tf_op jit(solution)/shard_map/stack | solution.py:62
  (6 shorter events, 0.0 us)
Async XLA Ops:
  0.6 27.6 %collective-permute-start = (f32[64,128]{1,0:T(8,128)}, f32[64,128]{1,0:T(8,128)S(1)}, u32[]{:S(2)}, u32[]{:S(2)}) collective-permute-start(f32[64,128]{1,0:T(8,128)} %param.3), channel_id=1, source_target_pairs={{0,1},{1,2},{2,3},{3,0},{4,5},{5,6},{6,7},{7,4},{8,9},{9,10},{10,1... | collective-permute-start | bytes 98312 | tf_op jit(solution)/shard_map/ppermute | solution.py:16
  1.1 27.2 %collective-permute-start.1 = (f32[64,128]{1,0:T(8,128)}, f32[64,128]{1,0:T(8,128)S(1)}, u32[]{:S(2)}, u32[]{:S(2)}) collective-permute-start(f32[64,128]{1,0:T(8,128)} %param.3), channel_id=1, source_target_pairs={{0,3},{1,0},{2,1},{3,2},{4,7},{5,4},{6,5},{7,6},{8,11},{9,8},{10,9... | collective-permute-start | bytes 98312 | tf_op jit(solution)/shard_map/ppermute | solution.py:21
  9.1 16.9 %copy-start.2 = (f32[64,128]{1,0:T(8,128)S(1)}, f32[64,128]{1,0:T(8,128)}, u32[]{:S(2)}) copy-start(f32[64,128]{1,0:T(8,128)} %param.3) | copy-start | bytes 98308
  26.0 1.9 %copy-start = (s32[128,2048]{1,0:T(8,128)S(1)}, s32[128,2048]{1,0:T(8,128)}, u32[]{:S(2)}) copy-start(s32[128,2048]{1,0:T(8,128)} %param.5) | copy-start | bytes 3145732
  28.3 3.4 %collective-permute-start.2 = (f32[64,128]{1,0:T(8,128)S(1)}, f32[64,128]{1,0:T(8,128)S(1)}, u32[]{:S(2)}, u32[]{:S(2)}) collective-permute-start(f32[64,128]{1,0:T(8,128)S(1)} %collective-permute-done), channel_id=1, source_target_pairs={{0,1},{1,2},{2,3},{3,0},{4,5},{5,6},{6,7},{7,4},{8,9},{9,10},{10,1... | collective-permute-start | bytes 98312 | tf_op jit(solution)/shard_map/ppermute | solution.py:16
  47.3 1.8 %copy-start.1 = (f32[64,128]{1,0:T(8,128)S(1)}, f32[64,128]{1,0:T(8,128)}, u32[]{:S(2)}) copy-start(f32[64,128]{1,0:T(8,128)} %param.4) | copy-start | bytes 98308
